TPU v7x, 32 devices: a whole 2x2x4 slice. The times are simulated.
32 devices in a mesh: section: 4 (over z), row: 8 (over y, x, core).
Axes of the slice: x: 2, y: 2, z: 4, core: 2. Of those that a mesh axis runs over, the one named last changes fastest.
Arguments:
- features: bfloat16 [16, 16, 16, 192], P(None, 'row'), may hold values from -6 to 6
- norm_gain: float32 [4, 192], P('section'), may hold values from 0.5 to 1.5
- conv_weight: bfloat16 [4, 3, 3, 3, 192, 192], P('section'), may hold values from -0.078125 to 0.078125
- conv_bias: float32 [4, 192], P('section'), may hold values from -2.5 to 2.5
Outputs:
- decoded: bfloat16 [16, 16, 16, 192], P('section', 'row')
All inputs are finite; a program needn't handle non-finite values.
Results may differ from a plain program's by a relative error of at most 0.03.
Values may be sent and summed in bfloat16 or wider, within the bound.
A program may use at most 64 MiB of HBM per device.

v0:
```python
import jax
import jax.numpy as jnp
from jax import lax
from jax.sharding import PartitionSpec as P

FRAMES = 4


def with_halo(block, sides, width):
    for axis, dim in sides:
        count = lax.axis_size(axis)
        forward = [(i, i + 1) for i in range(count - 1)]
        backward = [(target, source) for source, target in forward]
        low = lax.ppermute(
            lax.slice_in_dim(block, block.shape[dim] - width, None, axis=dim), axis, forward
        )
        high = lax.ppermute(lax.slice_in_dim(block, 0, width, axis=dim), axis, backward)
        block = jnp.concatenate([low, block, high], axis=dim)
    return block


def shifted(value, axis, steps):
    count = lax.axis_size(axis)
    first, last = (max(0, -steps), min(count, count - steps))
    return lax.ppermute(value, axis, [(source, source + steps) for source in range(first, last)])


def on_device(features, norm_gain, conv_weight, conv_bias):
    sections = lax.axis_size("section")
    place = lax.axis_index("section")
    frames_all, rows_dev, cols, chans = features.shape
    group = 2
    span = group * FRAMES
    batches = sections // group
    turns = batches + sections - 1
    blocks = features.reshape(batches, span, rows_dev, cols, chans)
    gain = norm_gain[0]
    bias = conv_bias[0]
    taps = conv_weight[0].reshape(3, 9 * chans, chans)

    def activate(state):
        wide = state.astype(jnp.float32)
        square = jnp.mean(wide * wide, axis=-1, keepdims=True)
        return jax.nn.silu(wide * lax.rsqrt(square + 1e-06) * gain).astype(jnp.bfloat16)

    def convolve(padded, state):
        framed = jnp.pad(padded, ((0, 0), (0, 0), (1, 1), (0, 0)))
        total = jnp.zeros((span * rows_dev * cols, chans), jnp.float32)
        for delay in range(3):
            window = framed[delay : delay + span]
            pieces = [
                window[:, dy : dy + rows_dev, dx : dx + cols] for dy in range(3) for dx in range(3)
            ]
            stacked = jnp.concatenate(pieces, axis=-1).reshape(-1, 9 * chans)
            total = total + jnp.dot(stacked, taps[delay], preferred_element_type=jnp.float32)
        result = state.astype(jnp.float32) + total.reshape(span, rows_dev, cols, chans) + bias
        return result.astype(jnp.bfloat16)

    memory = jnp.zeros((2, rows_dev, cols, chans), jnp.bfloat16)
    incoming = jnp.zeros((span, rows_dev, cols, chans), jnp.bfloat16)
    finished = jnp.zeros((batches, span, rows_dev, cols, chans), jnp.bfloat16)

    def advance(carry, turn):
        incoming, memory, finished = carry
        batch = turn - place
        active = jnp.logical_and(batch >= 0, batch < batches)
        slot = jnp.clip(batch, 0, batches - 1)
        own = lax.dynamic_index_in_dim(blocks, jnp.clip(turn, 0, batches - 1), 0, keepdims=False)
        state = jnp.where(place == 0, own, incoming)
        normed = activate(state)
        joined = jnp.concatenate([memory, normed], axis=0)
        padded = with_halo(joined, (("row", 1),), 1)
        renewed = normed[-2:]
        memory = jnp.where(active, renewed, memory)
        output = lax.cond(active, lambda: convolve(padded, state), lambda: state)
        keeping = jnp.logical_and(active, place == sections - 1)
        finished = jnp.where(
            keeping, lax.dynamic_update_index_in_dim(finished, output, slot, 0), finished
        )
        incoming = shifted(output, "section", 1)
        return ((incoming, memory, finished), None)

    carry, unused = lax.scan(advance, (incoming, memory, finished), jnp.arange(turns))
    finished = carry[2].reshape(sections, 1, FRAMES, rows_dev, cols, chans)
    received = lax.all_to_all(finished, "section", split_axis=0, concat_axis=1, tiled=True)
    return received[0, sections - 1]


def solution(mesh):
    in_specs = (
        P(None, "row", None, None),
        P("section", None),
        P("section", None, None, None, None, None),
        P("section", None),
    )
    out_specs = P("section", "row", None, None)
    return jax.shard_map(
        on_device, mesh=mesh, in_specs=in_specs, out_specs=out_specs, check_vma=False
    )
```

profile of v0, /device:TPU:2, one launch (start us, length us, event | category | flops | bytes accessed | tf_op | source)
XLA Modules:
  0.0 166.4 jit_solution(8224347381871252293)
XLA Ops:
  0.7 140.7 %while.16 = (s32[]{:T(128)}, bf16[8,2,16,192]{3,2,1,0:T(8,128)(2,1)S(1)}, bf16[2,2,16,192]{3,2,1,0:T(8,128)(2,1)}, bf16[2,8,2,16,192]{4,3,2,1,0:T(8,128)(2,1)}, ...) while((s32[]{:T(128)}, ...), condition=%wide.region_4.5_spmd.clone, body=%wide.region_0.4_spmd.clone.sunk | while | flops 510996736 | bytes 19456960 | solution.py:83
  5.2 1.9 %collective-permute-start = (bf16[10,1,16,192]{3,2,1,0:T(8,128)(2,1)S(1)}, bf16[10,1,16,192]{3,2,1,0:T(8,128)(2,1)S(1)}, u32[]{:S(2)}, u32[]{:S(2)}) collective-permute-start(bf16[10,1,16,192]{3,2,1,0:T(8,128)(2,1)S(1)} %get-tuple-element.311), channel_id=1, source_target_pairs={{1,0},{2,1},{3,2},{4,3},{5,4},{6,5},{7,6},{9,8},{10,9},{11,10},{12... | collective-permute-start | bytes 184328 | tf_op jit(solution)/shard_map/while/body/eval_jaxpr/ppermute | solution.py:17
  7.1 2.4 %collective-permute-start.1 = (bf16[10,1,16,192]{3,2,1,0:T(8,128)(2,1)S(1)}, bf16[10,1,16,192]{3,2,1,0:T(8,128)(2,1)S(1)}, u32[]{:S(2)}, u32[]{:S(2)}) collective-permute-start(bf16[10,1,16,192]{3,2,1,0:T(8,128)(2,1)S(1)} %get-tuple-element.312), channel_id=1, source_target_pairs={{0,1},{1,2},{2,3},{3,4},{4,5},{5,6},{6,7},{8,9},{9,10},{10,11},{11... | collective-permute-start | bytes 184328 | tf_op jit(solution)/shard_map/while/body/eval_jaxpr/ppermute | solution.py:14
  9.6 3.3 %collective-permute-done.1 = bf16[10,1,16,192]{3,2,1,0:T(8,128)(2,1)S(1)} collective-permute-done((bf16[10,1,16,192]{3,2,1,0:T(8,128)(2,1)S(1)}, bf16[10,1,16,192]{3,2,1,0:T(8,128)(2,1)S(1)}, u32[]{:S(2)}, u32[]{:S(2)}) %collective-permute-start.1) | collective-permute-done | bytes 61472 | tf_op jit(solution)/shard_map/while/body/eval_jaxpr/ppermute | solution.py:14
  13.0 10.9 %conditional.3 = (bf16[8,2,16,192]{3,2,1,0:T(8,128)(2,1)S(1)}) conditional(s32[]{:T(128)} %convert_element_type.53, bf16[8,2,16,192]{3,2,1,0:T(8,128)(2,1)S(1)} %get-tuple-element.308, (bf16[8,2,16,192]{3,2,1,0:T(8,128)(2,1)S(1)}, bf16[10,4,16,192]{3,2,1,0:T(8,128)(2,1)S(1)}, bf16[3,1728,192]{2,1,0:T(8,128)(2,1)}, f32[1,192]{1,0:T(1,128)}) %tuple.80), branch_computations={%region_2.2_spmd, %region_3.3_spmd} | conditional | flops 509902848 | bytes 16879396 | solution.py:75
  17.2 1.7 %fusion.2 = f32[256,192]{0,1:T(8,128)S(1)} fusion(bf16[256,1728]{1,0:T(8,128)(2,1)S(1)} %bitcast.40, bf16[3,1728,192]{2,1,0:T(8,128)(2,1)} %get-tuple-element.112), kind=kOutput, calls=%fused_computation.22 | convolution fusion | flops 169869312 | bytes 1966080 | tf_op jit(solution)/shard_map/while/body/eval_jaxpr/cond/branch_1_fun/dot_general | solution.py:55
  20.3 1.7 %convolution_add_fusion.1 = f32[256,192]{0,1:T(8,128)S(1)} fusion(f32[256,192]{0,1:T(8,128)S(1)} %fusion.2, bf16[256,1728]{1,0:T(8,128)(2,1)S(1)} %bitcast.39, bf16[3,1728,192]{2,1,0:T(8,128)(2,1)} %get-tuple-element.112), kind=kOutput, calls=%fused_computation.1 | convolution fusion | flops 169918464 | bytes 2162688 | tf_op jit(solution)/shard_map/while/body/eval_jaxpr/cond/branch_1_fun/dot_general | solution.py:55
  22.0 1.7 %convolution_add_fusion = f32[256,192]{0,1:T(8,128)S(1)} fusion(f32[256,192]{0,1:T(8,128)S(1)} %convolution_add_fusion.1, bf16[256,1728]{1,0:T(8,128)(2,1)S(1)} %bitcast.38, bf16[3,1728,192]{2,1,0:T(8,128)(2,1)} %get-tuple-element.112), kind=kOutput, calls=%fused_computation | convolution fusion | flops 169918464 | bytes 2162688 | tf_op jit(solution)/shard_map/while/body/eval_jaxpr/cond/branch_1_fun/dot_general | solution.py:55
  33.7 1.9 %collective-permute-start = (bf16[10,1,16,192]{3,2,1,0:T(8,128)(2,1)S(1)}, bf16[10,1,16,192]{3,2,1,0:T(8,128)(2,1)S(1)}, u32[]{:S(2)}, u32[]{:S(2)}) collective-permute-start(bf16[10,1,16,192]{3,2,1,0:T(8,128)(2,1)S(1)} %get-tuple-element.311), channel_id=1, source_target_pairs={{1,0},{2,1},{3,2},{4,3},{5,4},{6,5},{7,6},{9,8},{10,9},{11,10},{12... | collective-permute-start | bytes 184328 | tf_op jit(solution)/shard_map/while/body/eval_jaxpr/ppermute | solution.py:17
  35.6 2.4 %collective-permute-start.1 = (bf16[10,1,16,192]{3,2,1,0:T(8,128)(2,1)S(1)}, bf16[10,1,16,192]{3,2,1,0:T(8,128)(2,1)S(1)}, u32[]{:S(2)}, u32[]{:S(2)}) collective-permute-start(bf16[10,1,16,192]{3,2,1,0:T(8,128)(2,1)S(1)} %get-tuple-element.312), channel_id=1, source_target_pairs={{0,1},{1,2},{2,3},{3,4},{4,5},{5,6},{6,7},{8,9},{9,10},{10,11},{11... | collective-permute-start | bytes 184328 | tf_op jit(solution)/shard_map/while/body/eval_jaxpr/ppermute | solution.py:14
  38.0 3.3 %collective-permute-done.1 = bf16[10,1,16,192]{3,2,1,0:T(8,128)(2,1)S(1)} collective-permute-done((bf16[10,1,16,192]{3,2,1,0:T(8,128)(2,1)S(1)}, bf16[10,1,16,192]{3,2,1,0:T(8,128)(2,1)S(1)}, u32[]{:S(2)}, u32[]{:S(2)}) %collective-permute-start.1) | collective-permute-done | bytes 61472 | tf_op jit(solution)/shard_map/while/body/eval_jaxpr/ppermute | solution.py:14
  41.4 10.9 %conditional.3 = (bf16[8,2,16,192]{3,2,1,0:T(8,128)(2,1)S(1)}) conditional(s32[]{:T(128)} %convert_element_type.53, bf16[8,2,16,192]{3,2,1,0:T(8,128)(2,1)S(1)} %get-tuple-element.308, (bf16[8,2,16,192]{3,2,1,0:T(8,128)(2,1)S(1)}, bf16[10,4,16,192]{3,2,1,0:T(8,128)(2,1)S(1)}, bf16[3,1728,192]{2,1,0:T(8,128)(2,1)}, f32[1,192]{1,0:T(1,128)}) %tuple.80), branch_computations={%region_2.2_spmd, %region_3.3_spmd} | conditional | flops 509902848 | bytes 16879396 | solution.py:75
  45.7 1.7 %fusion.2 = f32[256,192]{0,1:T(8,128)S(1)} fusion(bf16[256,1728]{1,0:T(8,128)(2,1)S(1)} %bitcast.40, bf16[3,1728,192]{2,1,0:T(8,128)(2,1)} %get-tuple-element.112), kind=kOutput, calls=%fused_computation.22 | convolution fusion | flops 169869312 | bytes 1966080 | tf_op jit(solution)/shard_map/while/body/eval_jaxpr/cond/branch_1_fun/dot_general | solution.py:55
  48.7 1.7 %convolution_add_fusion.1 = f32[256,192]{0,1:T(8,128)S(1)} fusion(f32[256,192]{0,1:T(8,128)S(1)} %fusion.2, bf16[256,1728]{1,0:T(8,128)(2,1)S(1)} %bitcast.39, bf16[3,1728,192]{2,1,0:T(8,128)(2,1)} %get-tuple-element.112), kind=kOutput, calls=%fused_computation.1 | convolution fusion | flops 169918464 | bytes 2162688 | tf_op jit(solution)/shard_map/while/body/eval_jaxpr/cond/branch_1_fun/dot_general | solution.py:55
  50.4 1.7 %convolution_add_fusion = f32[256,192]{0,1:T(8,128)S(1)} fusion(f32[256,192]{0,1:T(8,128)S(1)} %convolution_add_fusion.1, bf16[256,1728]{1,0:T(8,128)(2,1)S(1)} %bitcast.38, bf16[3,1728,192]{2,1,0:T(8,128)(2,1)} %get-tuple-element.112), kind=kOutput, calls=%fused_computation | convolution fusion | flops 169918464 | bytes 2162688 | tf_op jit(solution)/shard_map/while/body/eval_jaxpr/cond/branch_1_fun/dot_general | solution.py:55
  52.3 4.4 %collective-permute-start.2 = (bf16[8,2,16,192]{3,2,1,0:T(8,128)(2,1)S(1)}, bf16[8,2,16,192]{3,2,1,0:T(8,128)(2,1)S(1)}, u32[]{:S(2)}, u32[]{:S(2)}) collective-permute-start(bf16[8,2,16,192]{3,2,1,0:T(8,128)(2,1)S(1)} %get-tuple-element.359), channel_id=1, source_target_pairs={{0,8},{8,16},{16,24},{1,9},{9,17},{17,25},{2,10},{10,18},{18,26},{... | collective-permute-start | bytes 294920 | tf_op jit(solution)/shard_map/while/body/eval_jaxpr/ppermute | solution.py:25
  65.0 1.9 %collective-permute-start = (bf16[10,1,16,192]{3,2,1,0:T(8,128)(2,1)S(1)}, bf16[10,1,16,192]{3,2,1,0:T(8,128)(2,1)S(1)}, u32[]{:S(2)}, u32[]{:S(2)}) collective-permute-start(bf16[10,1,16,192]{3,2,1,0:T(8,128)(2,1)S(1)} %get-tuple-element.311), channel_id=1, source_target_pairs={{1,0},{2,1},{3,2},{4,3},{5,4},{6,5},{7,6},{9,8},{10,9},{11,10},{12... | collective-permute-start | bytes 184328 | tf_op jit(solution)/shard_map/while/body/eval_jaxpr/ppermute | solution.py:17
  66.9 2.4 %collective-permute-start.1 = (bf16[10,1,16,192]{3,2,1,0:T(8,128)(2,1)S(1)}, bf16[10,1,16,192]{3,2,1,0:T(8,128)(2,1)S(1)}, u32[]{:S(2)}, u32[]{:S(2)}) collective-permute-start(bf16[10,1,16,192]{3,2,1,0:T(8,128)(2,1)S(1)} %get-tuple-element.312), channel_id=1, source_target_pairs={{0,1},{1,2},{2,3},{3,4},{4,5},{5,6},{6,7},{8,9},{9,10},{10,11},{11... | collective-permute-start | bytes 184328 | tf_op jit(solution)/shard_map/while/body/eval_jaxpr/ppermute | solution.py:14
  69.4 3.3 %collective-permute-done.1 = bf16[10,1,16,192]{3,2,1,0:T(8,128)(2,1)S(1)} collective-permute-done((bf16[10,1,16,192]{3,2,1,0:T(8,128)(2,1)S(1)}, bf16[10,1,16,192]{3,2,1,0:T(8,128)(2,1)S(1)}, u32[]{:S(2)}, u32[]{:S(2)}) %collective-permute-start.1) | collective-permute-done | bytes 61472 | tf_op jit(solution)/shard_map/while/body/eval_jaxpr/ppermute | solution.py:14
  72.8 15.3 %collective-permute-start.2 = (bf16[8,2,16,192]{3,2,1,0:T(8,128)(2,1)S(1)}, bf16[8,2,16,192]{3,2,1,0:T(8,128)(2,1)S(1)}, u32[]{:S(2)}, u32[]{:S(2)}) collective-permute-start(bf16[8,2,16,192]{3,2,1,0:T(8,128)(2,1)S(1)} %get-tuple-element.359), channel_id=1, source_target_pairs={{0,8},{8,16},{16,24},{1,9},{9,17},{17,25},{2,10},{10,18},{18,26},{... | collective-permute-start | bytes 294920 | tf_op jit(solution)/shard_map/while/body/eval_jaxpr/ppermute | solution.py:25
  89.7 1.8 %collective-permute-done.2 = bf16[8,2,16,192]{3,2,1,0:T(8,128)(2,1)S(1)} collective-permute-done((bf16[8,2,16,192]{3,2,1,0:T(8,128)(2,1)S(1)}, bf16[8,2,16,192]{3,2,1,0:T(8,128)(2,1)S(1)}, u32[]{:S(2)}, u32[]{:S(2)}) %collective-permute-start.2) | collective-permute-done | bytes 98336 | tf_op jit(solution)/shard_map/while/body/eval_jaxpr/ppermute | solution.py:25
  96.7 1.9 %collective-permute-start = (bf16[10,1,16,192]{3,2,1,0:T(8,128)(2,1)S(1)}, bf16[10,1,16,192]{3,2,1,0:T(8,128)(2,1)S(1)}, u32[]{:S(2)}, u32[]{:S(2)}) collective-permute-start(bf16[10,1,16,192]{3,2,1,0:T(8,128)(2,1)S(1)} %get-tuple-element.311), channel_id=1, source_target_pairs={{1,0},{2,1},{3,2},{4,3},{5,4},{6,5},{7,6},{9,8},{10,9},{11,10},{12... | collective-permute-start | bytes 184328 | tf_op jit(solution)/shard_map/while/body/eval_jaxpr/ppermute | solution.py:17
  98.6 2.4 %collective-permute-start.1 = (bf16[10,1,16,192]{3,2,1,0:T(8,128)(2,1)S(1)}, bf16[10,1,16,192]{3,2,1,0:T(8,128)(2,1)S(1)}, u32[]{:S(2)}, u32[]{:S(2)}) collective-permute-start(bf16[10,1,16,192]{3,2,1,0:T(8,128)(2,1)S(1)} %get-tuple-element.312), channel_id=1, source_target_pairs={{0,1},{1,2},{2,3},{3,4},{4,5},{5,6},{6,7},{8,9},{9,10},{10,11},{11... | collective-permute-start | bytes 184328 | tf_op jit(solution)/shard_map/while/body/eval_jaxpr/ppermute | solution.py:14
  101.0 3.3 %collective-permute-done.1 = bf16[10,1,16,192]{3,2,1,0:T(8,128)(2,1)S(1)} collective-permute-done((bf16[10,1,16,192]{3,2,1,0:T(8,128)(2,1)S(1)}, bf16[10,1,16,192]{3,2,1,0:T(8,128)(2,1)S(1)}, u32[]{:S(2)}, u32[]{:S(2)}) %collective-permute-start.1) | collective-permute-done | bytes 61472 | tf_op jit(solution)/shard_map/while/body/eval_jaxpr/ppermute | solution.py:14
  104.4 4.4 %collective-permute-start.2 = (bf16[8,2,16,192]{3,2,1,0:T(8,128)(2,1)S(1)}, bf16[8,2,16,192]{3,2,1,0:T(8,128)(2,1)S(1)}, u32[]{:S(2)}, u32[]{:S(2)}) collective-permute-start(bf16[8,2,16,192]{3,2,1,0:T(8,128)(2,1)S(1)} %get-tuple-element.359), channel_id=1, source_target_pairs={{0,8},{8,16},{16,24},{1,9},{9,17},{17,25},{2,10},{10,18},{18,26},{... | collective-permute-start | bytes 294920 | tf_op jit(solution)/shard_map/while/body/eval_jaxpr/ppermute | solution.py:25
  110.4 1.8 %collective-permute-done.2 = bf16[8,2,16,192]{3,2,1,0:T(8,128)(2,1)S(1)} collective-permute-done((bf16[8,2,16,192]{3,2,1,0:T(8,128)(2,1)S(1)}, bf16[8,2,16,192]{3,2,1,0:T(8,128)(2,1)S(1)}, u32[]{:S(2)}, u32[]{:S(2)}) %collective-permute-start.2) | collective-permute-done | bytes 98336 | tf_op jit(solution)/shard_map/while/body/eval_jaxpr/ppermute | solution.py:25
  117.4 1.9 %collective-permute-start = (bf16[10,1,16,192]{3,2,1,0:T(8,128)(2,1)S(1)}, bf16[10,1,16,192]{3,2,1,0:T(8,128)(2,1)S(1)}, u32[]{:S(2)}, u32[]{:S(2)}) collective-permute-start(bf16[10,1,16,192]{3,2,1,0:T(8,128)(2,1)S(1)} %get-tuple-element.311), channel_id=1, source_target_pairs={{1,0},{2,1},{3,2},{4,3},{5,4},{6,5},{7,6},{9,8},{10,9},{11,10},{12... | collective-permute-start | bytes 184328 | tf_op jit(solution)/shard_map/while/body/eval_jaxpr/ppermute | solution.py:17
  119.3 2.4 %collective-permute-start.1 = (bf16[10,1,16,192]{3,2,1,0:T(8,128)(2,1)S(1)}, bf16[10,1,16,192]{3,2,1,0:T(8,128)(2,1)S(1)}, u32[]{:S(2)}, u32[]{:S(2)}) collective-permute-start(bf16[10,1,16,192]{3,2,1,0:T(8,128)(2,1)S(1)} %get-tuple-element.312), channel_id=1, source_target_pairs={{0,1},{1,2},{2,3},{3,4},{4,5},{5,6},{6,7},{8,9},{9,10},{10,11},{11... | collective-permute-start | bytes 184328 | tf_op jit(solution)/shard_map/while/body/eval_jaxpr/ppermute | solution.py:14
  121.8 3.3 %collective-permute-done.1 = bf16[10,1,16,192]{3,2,1,0:T(8,128)(2,1)S(1)} collective-permute-done((bf16[10,1,16,192]{3,2,1,0:T(8,128)(2,1)S(1)}, bf16[10,1,16,192]{3,2,1,0:T(8,128)(2,1)S(1)}, u32[]{:S(2)}, u32[]{:S(2)}) %collective-permute-start.1) | collective-permute-done | bytes 61472 | tf_op jit(solution)/shard_map/while/body/eval_jaxpr/ppermute | solution.py:14
  125.2 12.8 %collective-permute-start.2 = (bf16[8,2,16,192]{3,2,1,0:T(8,128)(2,1)S(1)}, bf16[8,2,16,192]{3,2,1,0:T(8,128)(2,1)S(1)}, u32[]{:S(2)}, u32[]{:S(2)}) collective-permute-start(bf16[8,2,16,192]{3,2,1,0:T(8,128)(2,1)S(1)} %get-tuple-element.359), channel_id=1, source_target_pairs={{0,8},{8,16},{16,24},{1,9},{9,17},{17,25},{2,10},{10,18},{18,26},{... | collective-permute-start | bytes 294920 | tf_op jit(solution)/shard_map/while/body/eval_jaxpr/ppermute | solution.py:25
  139.6 1.8 %collective-permute-done.2 = bf16[8,2,16,192]{3,2,1,0:T(8,128)(2,1)S(1)} collective-permute-done((bf16[8,2,16,192]{3,2,1,0:T(8,128)(2,1)S(1)}, bf16[8,2,16,192]{3,2,1,0:T(8,128)(2,1)S(1)}, u32[]{:S(2)}, u32[]{:S(2)}) %collective-permute-start.2) | collective-permute-done | bytes 98336 | tf_op jit(solution)/shard_map/while/body/eval_jaxpr/ppermute | solution.py:25
  141.4 24.3 %all_to_all.12 = bf16[4,1,4,2,16,192]{5,4,3,2,1,0:T(8,128)(2,1)S(1)} all-to-all(bf16[4,1,4,2,16,192]{5,4,3,2,1,0:T(8,128)(2,1)} %bitcast.43), channel_id=1, replica_groups=mesh['section'=4,'row'=8] {'section'}, dimensions={0} | all-to-all | bytes 393216 | tf_op jit(solution)/shard_map/all_to_all | solution.py:85
  (74 shorter events, 44.4 us)
Async XLA Ops:
  5.2 4.4 %collective-permute-start = (bf16[10,1,16,192]{3,2,1,0:T(8,128)(2,1)S(1)}, bf16[10,1,16,192]{3,2,1,0:T(8,128)(2,1)S(1)}, u32[]{:S(2)}, u32[]{:S(2)}) collective-permute-start(bf16[10,1,16,192]{3,2,1,0:T(8,128)(2,1)S(1)} %get-tuple-element.311), channel_id=1, source_target_pairs={{1,0},{2,1},{3,2},{4,3},{5,4},{6,5},{7,6},{9,8},{10,9},{11,10},{12... | collective-permute-start | bytes 184328 | tf_op jit(solution)/shard_map/while/body/eval_jaxpr/ppermute | solution.py:17
  7.1 5.8 %collective-permute-start.1 = (bf16[10,1,16,192]{3,2,1,0:T(8,128)(2,1)S(1)}, bf16[10,1,16,192]{3,2,1,0:T(8,128)(2,1)S(1)}, u32[]{:S(2)}, u32[]{:S(2)}) collective-permute-start(bf16[10,1,16,192]{3,2,1,0:T(8,128)(2,1)S(1)} %get-tuple-element.312), channel_id=1, source_target_pairs={{0,1},{1,2},{2,3},{3,4},{4,5},{5,6},{6,7},{8,9},{9,10},{10,11},{11... | collective-permute-start | bytes 184328 | tf_op jit(solution)/shard_map/while/body/eval_jaxpr/ppermute | solution.py:14
  20.3 3.5 %copy-start = (f32[1,192]{1,0:T(1,128)S(1)}, f32[1,192]{1,0:T(1,128)}, u32[]{:S(2)}) copy-start(f32[1,192]{1,0:T(1,128)} %get-tuple-element.113) | copy-start | bytes 2308 | tf_op jit(solution)/shard_map/while/body/eval_jaxpr/cond
  23.9 4.6 %collective-permute-start.2 = (bf16[8,2,16,192]{3,2,1,0:T(8,128)(2,1)S(1)}, bf16[8,2,16,192]{3,2,1,0:T(8,128)(2,1)S(1)}, u32[]{:S(2)}, u32[]{:S(2)}) collective-permute-start(bf16[8,2,16,192]{3,2,1,0:T(8,128)(2,1)S(1)} %get-tuple-element.359), channel_id=1, source_target_pairs={{0,8},{8,16},{16,24},{1,9},{9,17},{17,25},{2,10},{10,18},{18,26},{... | collective-permute-start | bytes 294920 | tf_op jit(solution)/shard_map/while/body/eval_jaxpr/ppermute | solution.py:25
  33.7 4.4 %collective-permute-start = (bf16[10,1,16,192]{3,2,1,0:T(8,128)(2,1)S(1)}, bf16[10,1,16,192]{3,2,1,0:T(8,128)(2,1)S(1)}, u32[]{:S(2)}, u32[]{:S(2)}) collective-permute-start(bf16[10,1,16,192]{3,2,1,0:T(8,128)(2,1)S(1)} %get-tuple-element.311), channel_id=1, source_target_pairs={{1,0},{2,1},{3,2},{4,3},{5,4},{6,5},{7,6},{9,8},{10,9},{11,10},{12... | collective-permute-start | bytes 184328 | tf_op jit(solution)/shard_map/while/body/eval_jaxpr/ppermute | solution.py:17
  35.6 5.8 %collective-permute-start.1 = (bf16[10,1,16,192]{3,2,1,0:T(8,128)(2,1)S(1)}, bf16[10,1,16,192]{3,2,1,0:T(8,128)(2,1)S(1)}, u32[]{:S(2)}, u32[]{:S(2)}) collective-permute-start(bf16[10,1,16,192]{3,2,1,0:T(8,128)(2,1)S(1)} %get-tuple-element.312), channel_id=1, source_target_pairs={{0,1},{1,2},{2,3},{3,4},{4,5},{5,6},{6,7},{8,9},{9,10},{10,11},{11... | collective-permute-start | bytes 184328 | tf_op jit(solution)/shard_map/while/body/eval_jaxpr/ppermute | solution.py:14
  48.7 3.5 %copy-start = (f32[1,192]{1,0:T(1,128)S(1)}, f32[1,192]{1,0:T(1,128)}, u32[]{:S(2)}) copy-start(f32[1,192]{1,0:T(1,128)} %get-tuple-element.113) | copy-start | bytes 2308 | tf_op jit(solution)/shard_map/while/body/eval_jaxpr/cond
  52.3 7.5 %collective-permute-start.2 = (bf16[8,2,16,192]{3,2,1,0:T(8,128)(2,1)S(1)}, bf16[8,2,16,192]{3,2,1,0:T(8,128)(2,1)S(1)}, u32[]{:S(2)}, u32[]{:S(2)}) collective-permute-start(bf16[8,2,16,192]{3,2,1,0:T(8,128)(2,1)S(1)} %get-tuple-element.359), channel_id=1, source_target_pairs={{0,8},{8,16},{16,24},{1,9},{9,17},{17,25},{2,10},{10,18},{18,26},{... | collective-permute-start | bytes 294920 | tf_op jit(solution)/shard_map/while/body/eval_jaxpr/ppermute | solution.py:25
  65.0 4.4 %collective-permute-start = (bf16[10,1,16,192]{3,2,1,0:T(8,128)(2,1)S(1)}, bf16[10,1,16,192]{3,2,1,0:T(8,128)(2,1)S(1)}, u32[]{:S(2)}, u32[]{:S(2)}) collective-permute-start(bf16[10,1,16,192]{3,2,1,0:T(8,128)(2,1)S(1)} %get-tuple-element.311), channel_id=1, source_target_pairs={{1,0},{2,1},{3,2},{4,3},{5,4},{6,5},{7,6},{9,8},{10,9},{11,10},{12... | collective-permute-start | bytes 184328 | tf_op jit(solution)/shard_map/while/body/eval_jaxpr/ppermute | solution.py:17
  66.9 5.8 %collective-permute-start.1 = (bf16[10,1,16,192]{3,2,1,0:T(8,128)(2,1)S(1)}, bf16[10,1,16,192]{3,2,1,0:T(8,128)(2,1)S(1)}, u32[]{:S(2)}, u32[]{:S(2)}) collective-permute-start(bf16[10,1,16,192]{3,2,1,0:T(8,128)(2,1)S(1)} %get-tuple-element.312), channel_id=1, source_target_pairs={{0,1},{1,2},{2,3},{3,4},{4,5},{5,6},{6,7},{8,9},{9,10},{10,11},{11... | collective-permute-start | bytes 184328 | tf_op jit(solution)/shard_map/while/body/eval_jaxpr/ppermute | solution.py:14
  72.8 18.6 %collective-permute-start.2 = (bf16[8,2,16,192]{3,2,1,0:T(8,128)(2,1)S(1)}, bf16[8,2,16,192]{3,2,1,0:T(8,128)(2,1)S(1)}, u32[]{:S(2)}, u32[]{:S(2)}) collective-permute-start(bf16[8,2,16,192]{3,2,1,0:T(8,128)(2,1)S(1)} %get-tuple-element.359), channel_id=1, source_target_pairs={{0,8},{8,16},{16,24},{1,9},{9,17},{17,25},{2,10},{10,18},{18,26},{... | collective-permute-start | bytes 294920 | tf_op jit(solution)/shard_map/while/body/eval_jaxpr/ppermute | solution.py:25
  96.7 4.4 %collective-permute-start = (bf16[10,1,16,192]{3,2,1,0:T(8,128)(2,1)S(1)}, bf16[10,1,16,192]{3,2,1,0:T(8,128)(2,1)S(1)}, u32[]{:S(2)}, u32[]{:S(2)}) collective-permute-start(bf16[10,1,16,192]{3,2,1,0:T(8,128)(2,1)S(1)} %get-tuple-element.311), channel_id=1, source_target_pairs={{1,0},{2,1},{3,2},{4,3},{5,4},{6,5},{7,6},{9,8},{10,9},{11,10},{12... | collective-permute-start | bytes 184328 | tf_op jit(solution)/shard_map/while/body/eval_jaxpr/ppermute | solution.py:17
  98.6 5.8 %collective-permute-start.1 = (bf16[10,1,16,192]{3,2,1,0:T(8,128)(2,1)S(1)}, bf16[10,1,16,192]{3,2,1,0:T(8,128)(2,1)S(1)}, u32[]{:S(2)}, u32[]{:S(2)}) collective-permute-start(bf16[10,1,16,192]{3,2,1,0:T(8,128)(2,1)S(1)} %get-tuple-element.312), channel_id=1, source_target_pairs={{0,1},{1,2},{2,3},{3,4},{4,5},{5,6},{6,7},{8,9},{9,10},{10,11},{11... | collective-permute-start | bytes 184328 | tf_op jit(solution)/shard_map/while/body/eval_jaxpr/ppermute | solution.py:14
  104.4 7.8 %collective-permute-start.2 = (bf16[8,2,16,192]{3,2,1,0:T(8,128)(2,1)S(1)}, bf16[8,2,16,192]{3,2,1,0:T(8,128)(2,1)S(1)}, u32[]{:S(2)}, u32[]{:S(2)}) collective-permute-start(bf16[8,2,16,192]{3,2,1,0:T(8,128)(2,1)S(1)} %get-tuple-element.359), channel_id=1, source_target_pairs={{0,8},{8,16},{16,24},{1,9},{9,17},{17,25},{2,10},{10,18},{18,26},{... | collective-permute-start | bytes 294920 | tf_op jit(solution)/shard_map/while/body/eval_jaxpr/ppermute | solution.py:25
  117.4 4.4 %collective-permute-start = (bf16[10,1,16,192]{3,2,1,0:T(8,128)(2,1)S(1)}, bf16[10,1,16,192]{3,2,1,0:T(8,128)(2,1)S(1)}, u32[]{:S(2)}, u32[]{:S(2)}) collective-permute-start(bf16[10,1,16,192]{3,2,1,0:T(8,128)(2,1)S(1)} %get-tuple-element.311), channel_id=1, source_target_pairs={{1,0},{2,1},{3,2},{4,3},{5,4},{6,5},{7,6},{9,8},{10,9},{11,10},{12... | collective-permute-start | bytes 184328 | tf_op jit(solution)/shard_map/while/body/eval_jaxpr/ppermute | solution.py:17
  119.3 5.8 %collective-permute-start.1 = (bf16[10,1,16,192]{3,2,1,0:T(8,128)(2,1)S(1)}, bf16[10,1,16,192]{3,2,1,0:T(8,128)(2,1)S(1)}, u32[]{:S(2)}, u32[]{:S(2)}) collective-permute-start(bf16[10,1,16,192]{3,2,1,0:T(8,128)(2,1)S(1)} %get-tuple-element.312), channel_id=1, source_target_pairs={{0,1},{1,2},{2,3},{3,4},{4,5},{5,6},{6,7},{8,9},{9,10},{10,11},{11... | collective-permute-start | bytes 184328 | tf_op jit(solution)/shard_map/while/body/eval_jaxpr/ppermute | solution.py:14
  125.2 16.2 %collective-permute-start.2 = (bf16[8,2,16,192]{3,2,1,0:T(8,128)(2,1)S(1)}, bf16[8,2,16,192]{3,2,1,0:T(8,128)(2,1)S(1)}, u32[]{:S(2)}, u32[]{:S(2)}) collective-permute-start(bf16[8,2,16,192]{3,2,1,0:T(8,128)(2,1)S(1)} %get-tuple-element.359), channel_id=1, source_target_pairs={{0,8},{8,16},{16,24},{1,9},{9,17},{17,25},{2,10},{10,18},{18,26},{... | collective-permute-start | bytes 294920 | tf_op jit(solution)/shard_map/while/body/eval_jaxpr/ppermute | solution.py:25
where the time goes:
time: 168 us; the launch traced here: 166 us
  starting transfers between devices  59.8 us (36%)
  waiting for transfers between devices  25.1 us (15%)
  blocking collectives  24.3 us (14%)
  other arithmetic  24.1 us (14%)
  local copies, waits for them, and re-layouts  15.8 us (9%)
  matrix products  10.1 us (6%)
  loops' own time  7.08 us (4%)
    ppermute x5, starting transfers between devices, shifted(): lax.ppermute(value, axis, [(source, source + steps) for source in range(f...  38.2 us
    all_to_all x1, blocking collectives, on_device(): lax.all_to_all(finished, 'section', split_axis=0, concat_axis=1, tiled=True)  24.3 us
    ppermute x5, waiting for transfers between devices, with_halo(): lax.ppermute(lax.slice_in_dim(block, block.shape[dim] - width, None, axis...  16.6 us
    ppermute x5, starting transfers between devices, with_halo(): lax.ppermute(lax.slice_in_dim(block, block.shape[dim] - width, None, axis...  12 us
    dot_general x6, matrix products, convolve(): jnp.dot(stacked, taps[delay], preferred_element_type=jnp.float32)  10.1 us
    ppermute x5, starting transfers between devices, with_halo(): lax.ppermute(lax.slice_in_dim(block, 0, width, axis=dim), axis, backward)  9.6 us
    ppermute x5, waiting for transfers between devices, shifted(): lax.ppermute(value, axis, [(source, source + steps) for source in range(f...  8.46 us
    concatenate x6, local copies, waits for them, and re-layouts, convolve(): stacked = jnp.concatenate(pieces, axis=-1).reshape(-1, 9 * chans)  8.15 us
  transfers between devices with their start and end apart: 15, of which 10 were waited for; matrix products, arithmetic and copies ran while one was open for 5% of the time, Pallas kernels for 0%

commit v1 on v0

--- a/solution.py
+++ b/solution.py
@@ -4,6 +4,29 @@
 from jax.sharding import PartitionSpec as P
 
 FRAMES = 4
+
+
+def split_up(value, dim, size):
+    dims = value.shape
+    blocks = value.reshape(*dims[:dim], size, dims[dim] // size, *dims[dim + 1 :])
+    return jnp.moveaxis(blocks, dim, 0)
+
+
+def in_order(blocks, dim):
+    blocks = jnp.moveaxis(blocks, 0, dim)
+    dims = blocks.shape
+    return blocks.reshape(*dims[:dim], dims[dim] * dims[dim + 1], *dims[dim + 2 :])
+
+
+def exchange_in_pairs(x, axis, split_dim, concat_dim):
+    size, position = (lax.axis_size(axis), lax.axis_index(axis))
+    tiles = split_up(x, split_dim, size)
+    finished = [tiles[position]]
+    for lap in range(1, size):
+        sent = tiles[position ^ lap]
+        finished.append(lax.ppermute(sent, axis, [(i, i ^ lap) for i in range(size)]))
+    tiles = jnp.stack(finished)[position ^ jnp.arange(size)]
+    return in_order(tiles, concat_dim)
 
 
 def with_halo(block, sides, width):
@@ -82,7 +105,7 @@
 
     carry, unused = lax.scan(advance, (incoming, memory, finished), jnp.arange(turns))
     finished = carry[2].reshape(sections, 1, FRAMES, rows_dev, cols, chans)
-    received = lax.all_to_all(finished, "section", split_axis=0, concat_axis=1, tiled=True)
+    received = exchange_in_pairs(finished, "section", 0, 1)
     return received[0, sections - 1]
 
 

time: 168 us -> 160 us (0.952)
  blocking collectives: 24.3 us -> 0 us
  starting transfers between devices: 59.8 us -> 74.9 us
  other arithmetic: 24.1 us -> 18.1 us
  waiting for transfers between devices: 25.1 us -> 29.8 us
    all_to_all x1 -> x0, blocking collectives: 24.3 us -> none  [on_device(): lax.all_to_all(finished, 'section', split_axis=0, concat_axis=1, tiled=True)]
    ppermute x0 -> x3, starting transfers between devices: none -> 15.3 us  [exchange_in_pairs(): lax.ppermute(sent, axis, [(i, i ^ lap) for i in range(size)])]
    select_n x5, other arithmetic: 6.2 us -> 0.09 us  [advance(): memory = jnp.where(active, renewed, memory)]
    ppermute x0 -> x3, waiting for transfers between devices: none -> 4.69 us  [exchange_in_pairs(): lax.ppermute(sent, axis, [(i, i ^ lap) for i in range(size)])]
  transfers between devices with their start and end apart: 15 -> 18, of which waited for: 10 -> 13; matrix products, arithmetic and copies ran while one was open for 5% -> 5% of each run, Pallas kernels for 0% -> 0%
where the time goes in v1:
time: 160 us; the launch traced here: 157 us
  starting transfers between devices  74.9 us (47%)
  waiting for transfers between devices  29.8 us (19%)
  other arithmetic  18.1 us (11%)
  local copies, waits for them, and re-layouts  17.1 us (11%)
  matrix products  10.1 us (6%)
  loops' own time  7.07 us (4%)
    ppermute x5, starting transfers between devices, shifted(): lax.ppermute(value, axis, [(source, source + steps) for source in range(f...  38 us
    ppermute x5, waiting for transfers between devices, with_halo(): lax.ppermute(lax.slice_in_dim(block, block.shape[dim] - width, None, axis...  16.6 us
    ppermute x3, starting transfers between devices, exchange_in_pairs(): lax.ppermute(sent, axis, [(i, i ^ lap) for i in range(size)])  15.3 us
    ppermute x5, starting transfers between devices, with_halo(): lax.ppermute(lax.slice_in_dim(block, block.shape[dim] - width, None, axis...  12 us
    dot_general x6, matrix products, convolve(): jnp.dot(stacked, taps[delay], preferred_element_type=jnp.float32)  10.1 us
    ppermute x5, starting transfers between devices, with_halo(): lax.ppermute(lax.slice_in_dim(block, 0, width, axis=dim), axis, backward)  9.6 us
    ppermute x5, waiting for transfers between devices, shifted(): lax.ppermute(value, axis, [(source, source + steps) for source in range(f...  8.51 us
    select_n x5, other arithmetic, advance(): jnp.where(keeping, lax.dynamic_update_index_in_dim(finished, output, slot...  7.95 us
  transfers between devices with their start and end apart: 18, of which 13 were waited for; matrix products, arithmetic and copies ran while one was open for 5% of the time, Pallas kernels for 0%

profile of v1, /device:TPU:2, one launch (start us, length us, event | category | flops | bytes accessed | tf_op | source)
XLA Modules:
  0.0 157.2 jit_solution(6671306234099605103)
XLA Ops:
  0.7 134.2 %while.16 = (s32[]{:T(128)}, bf16[8,2,16,192]{3,2,1,0:T(8,128)(2,1)S(1)}, bf16[2,2,16,192]{3,2,1,0:T(8,128)(2,1)S(1)}, bf16[2,8,2,16,192]{4,3,2,1,0:T(8,128)(2,1...) while((s32[]{:T(128)}, ...), condition=%wide.region_4.5_spmd.clone, body=%wide.region_0.4_spmd.clone.sunk | while | flops 510996736 | bytes 19456960 | solution.py:106
  4.6 1.9 %collective-permute-start = (bf16[10,1,16,192]{3,2,1,0:T(8,128)(2,1)S(1)}, bf16[10,1,16,192]{3,2,1,0:T(8,128)(2,1)S(1)}, u32[]{:S(2)}, u32[]{:S(2)}) collective-permute-start(bf16[10,1,16,192]{3,2,1,0:T(8,128)(2,1)S(1)} %get-tuple-element.315), channel_id=1, source_target_pairs={{1,0},{2,1},{3,2},{4,3},{5,4},{6,5},{7,6},{9,8},{10,9},{11,10},{12... | collective-permute-start | bytes 184328 | tf_op jit(solution)/shard_map/while/body/eval_jaxpr/ppermute | solution.py:40
  6.5 2.4 %collective-permute-start.1 = (bf16[10,1,16,192]{3,2,1,0:T(8,128)(2,1)S(1)}, bf16[10,1,16,192]{3,2,1,0:T(8,128)(2,1)S(1)}, u32[]{:S(2)}, u32[]{:S(2)}) collective-permute-start(bf16[10,1,16,192]{3,2,1,0:T(8,128)(2,1)S(1)} %get-tuple-element.316), channel_id=1, source_target_pairs={{0,1},{1,2},{2,3},{3,4},{4,5},{5,6},{6,7},{8,9},{9,10},{10,11},{11... | collective-permute-start | bytes 184328 | tf_op jit(solution)/shard_map/while/body/eval_jaxpr/ppermute | solution.py:37
  9.0 3.3 %collective-permute-done.1 = bf16[10,1,16,192]{3,2,1,0:T(8,128)(2,1)S(1)} collective-permute-done((bf16[10,1,16,192]{3,2,1,0:T(8,128)(2,1)S(1)}, bf16[10,1,16,192]{3,2,1,0:T(8,128)(2,1)S(1)}, u32[]{:S(2)}, u32[]{:S(2)}) %collective-permute-start.1) | collective-permute-done | bytes 61472 | tf_op jit(solution)/shard_map/while/body/eval_jaxpr/ppermute | solution.py:37
  12.4 10.8 %conditional.3 = (bf16[8,2,16,192]{3,2,1,0:T(8,128)(2,1)S(1)}) conditional(s32[]{:T(128)} %convert_element_type.53, bf16[8,2,16,192]{3,2,1,0:T(8,128)(2,1)S(1)} %get-tuple-element.312, (bf16[8,2,16,192]{3,2,1,0:T(8,128)(2,1)S(1)}, bf16[10,4,16,192]{3,2,1,0:T(8,128)(2,1)S(1)}, bf16[3,1728,192]{2,1,0:T(8,128)(2,1)}, f32[1,192]{1,0:T(1,128)}) %tuple.83), branch_computations={%region_2.2_spmd, %region_3.3_spmd} | conditional | flops 509902848 | bytes 16879396 | solution.py:98
  16.0 1.7 %fusion.2 = f32[256,192]{0,1:T(8,128)S(1)} fusion(bf16[256,1728]{1,0:T(8,128)(2,1)S(1)} %bitcast.53, bf16[3,1728,192]{2,1,0:T(8,128)(2,1)} %get-tuple-element.112), kind=kOutput, calls=%fused_computation.23 | convolution fusion | flops 169869312 | bytes 1966080 | tf_op jit(solution)/shard_map/while/body/eval_jaxpr/cond/branch_1_fun/dot_general | solution.py:78
  21.3 1.7 %convolution_add_fusion = f32[256,192]{0,1:T(8,128)S(1)} fusion(f32[256,192]{0,1:T(8,128)S(1)} %convolution_add_fusion.1, bf16[256,1728]{1,0:T(8,128)(2,1)S(1)} %bitcast.52, bf16[3,1728,192]{2,1,0:T(8,128)(2,1)} %get-tuple-element.112), kind=kOutput, calls=%fused_computation.1 | convolution fusion | flops 169918464 | bytes 2162688 | tf_op jit(solution)/shard_map/while/body/eval_jaxpr/cond/branch_1_fun/dot_general | solution.py:78
  31.6 1.9 %collective-permute-start = (bf16[10,1,16,192]{3,2,1,0:T(8,128)(2,1)S(1)}, bf16[10,1,16,192]{3,2,1,0:T(8,128)(2,1)S(1)}, u32[]{:S(2)}, u32[]{:S(2)}) collective-permute-start(bf16[10,1,16,192]{3,2,1,0:T(8,128)(2,1)S(1)} %get-tuple-element.315), channel_id=1, source_target_pairs={{1,0},{2,1},{3,2},{4,3},{5,4},{6,5},{7,6},{9,8},{10,9},{11,10},{12... | collective-permute-start | bytes 184328 | tf_op jit(solution)/shard_map/while/body/eval_jaxpr/ppermute | solution.py:40
  33.5 2.4 %collective-permute-start.1 = (bf16[10,1,16,192]{3,2,1,0:T(8,128)(2,1)S(1)}, bf16[10,1,16,192]{3,2,1,0:T(8,128)(2,1)S(1)}, u32[]{:S(2)}, u32[]{:S(2)}) collective-permute-start(bf16[10,1,16,192]{3,2,1,0:T(8,128)(2,1)S(1)} %get-tuple-element.316), channel_id=1, source_target_pairs={{0,1},{1,2},{2,3},{3,4},{4,5},{5,6},{6,7},{8,9},{9,10},{10,11},{11... | collective-permute-start | bytes 184328 | tf_op jit(solution)/shard_map/while/body/eval_jaxpr/ppermute | solution.py:37
  35.9 3.3 %collective-permute-done.1 = bf16[10,1,16,192]{3,2,1,0:T(8,128)(2,1)S(1)} collective-permute-done((bf16[10,1,16,192]{3,2,1,0:T(8,128)(2,1)S(1)}, bf16[10,1,16,192]{3,2,1,0:T(8,128)(2,1)S(1)}, u32[]{:S(2)}, u32[]{:S(2)}) %collective-permute-start.1) | collective-permute-done | bytes 61472 | tf_op jit(solution)/shard_map/while/body/eval_jaxpr/ppermute | solution.py:37
  39.3 10.8 %conditional.3 = (bf16[8,2,16,192]{3,2,1,0:T(8,128)(2,1)S(1)}) conditional(s32[]{:T(128)} %convert_element_type.53, bf16[8,2,16,192]{3,2,1,0:T(8,128)(2,1)S(1)} %get-tuple-element.312, (bf16[8,2,16,192]{3,2,1,0:T(8,128)(2,1)S(1)}, bf16[10,4,16,192]{3,2,1,0:T(8,128)(2,1)S(1)}, bf16[3,1728,192]{2,1,0:T(8,128)(2,1)}, f32[1,192]{1,0:T(1,128)}) %tuple.83), branch_computations={%region_2.2_spmd, %region_3.3_spmd} | conditional | flops 509902848 | bytes 16879396 | solution.py:98
  46.0 1.7 %convolution_add_fusion.1 = f32[256,192]{0,1:T(8,128)S(1)} fusion(f32[256,192]{0,1:T(8,128)S(1)} %fusion.2, bf16[256,1728]{1,0:T(8,128)(2,1)S(1)} %bitcast.51, bf16[3,1728,192]{2,1,0:T(8,128)(2,1)} %get-tuple-element.112), kind=kOutput, calls=%fused_computation.2 | convolution fusion | flops 169918464 | bytes 2162688 | tf_op jit(solution)/shard_map/while/body/eval_jaxpr/cond/branch_1_fun/dot_general | solution.py:78
  48.2 1.7 %convolution_add_fusion = f32[256,192]{0,1:T(8,128)S(1)} fusion(f32[256,192]{0,1:T(8,128)S(1)} %convolution_add_fusion.1, bf16[256,1728]{1,0:T(8,128)(2,1)S(1)} %bitcast.52, bf16[3,1728,192]{2,1,0:T(8,128)(2,1)} %get-tuple-element.112), kind=kOutput, calls=%fused_computation.1 | convolution fusion | flops 169918464 | bytes 2162688 | tf_op jit(solution)/shard_map/while/body/eval_jaxpr/cond/branch_1_fun/dot_general | solution.py:78
  50.1 4.4 %collective-permute-start.2 = (bf16[8,2,16,192]{3,2,1,0:T(8,128)(2,1)S(1)}, bf16[8,2,16,192]{3,2,1,0:T(8,128)(2,1)S(1)}, u32[]{:S(2)}, u32[]{:S(2)}) collective-permute-start(bf16[8,2,16,192]{3,2,1,0:T(8,128)(2,1)S(1)} %get-tuple-element.363), channel_id=1, source_target_pairs={{0,8},{8,16},{16,24},{1,9},{9,17},{17,25},{2,10},{10,18},{18,26},{... | collective-permute-start | bytes 294920 | tf_op jit(solution)/shard_map/while/body/eval_jaxpr/ppermute | solution.py:48
  61.5 1.9 %collective-permute-start = (bf16[10,1,16,192]{3,2,1,0:T(8,128)(2,1)S(1)}, bf16[10,1,16,192]{3,2,1,0:T(8,128)(2,1)S(1)}, u32[]{:S(2)}, u32[]{:S(2)}) collective-permute-start(bf16[10,1,16,192]{3,2,1,0:T(8,128)(2,1)S(1)} %get-tuple-element.315), channel_id=1, source_target_pairs={{1,0},{2,1},{3,2},{4,3},{5,4},{6,5},{7,6},{9,8},{10,9},{11,10},{12... | collective-permute-start | bytes 184328 | tf_op jit(solution)/shard_map/while/body/eval_jaxpr/ppermute | solution.py:40
  63.4 2.4 %collective-permute-start.1 = (bf16[10,1,16,192]{3,2,1,0:T(8,128)(2,1)S(1)}, bf16[10,1,16,192]{3,2,1,0:T(8,128)(2,1)S(1)}, u32[]{:S(2)}, u32[]{:S(2)}) collective-permute-start(bf16[10,1,16,192]{3,2,1,0:T(8,128)(2,1)S(1)} %get-tuple-element.316), channel_id=1, source_target_pairs={{0,1},{1,2},{2,3},{3,4},{4,5},{5,6},{6,7},{8,9},{9,10},{10,11},{11... | collective-permute-start | bytes 184328 | tf_op jit(solution)/shard_map/while/body/eval_jaxpr/ppermute | solution.py:37
  65.8 3.3 %collective-permute-done.1 = bf16[10,1,16,192]{3,2,1,0:T(8,128)(2,1)S(1)} collective-permute-done((bf16[10,1,16,192]{3,2,1,0:T(8,128)(2,1)S(1)}, bf16[10,1,16,192]{3,2,1,0:T(8,128)(2,1)S(1)}, u32[]{:S(2)}, u32[]{:S(2)}) %collective-permute-start.1) | collective-permute-done | bytes 61472 | tf_op jit(solution)/shard_map/while/body/eval_jaxpr/ppermute | solution.py:37
  69.2 15.2 %collective-permute-start.2 = (bf16[8,2,16,192]{3,2,1,0:T(8,128)(2,1)S(1)}, bf16[8,2,16,192]{3,2,1,0:T(8,128)(2,1)S(1)}, u32[]{:S(2)}, u32[]{:S(2)}) collective-permute-start(bf16[8,2,16,192]{3,2,1,0:T(8,128)(2,1)S(1)} %get-tuple-element.363), channel_id=1, source_target_pairs={{0,8},{8,16},{16,24},{1,9},{9,17},{17,25},{2,10},{10,18},{18,26},{... | collective-permute-start | bytes 294920 | tf_op jit(solution)/shard_map/while/body/eval_jaxpr/ppermute | solution.py:48
  86.0 1.8 %collective-permute-done.2 = bf16[8,2,16,192]{3,2,1,0:T(8,128)(2,1)S(1)} collective-permute-done((bf16[8,2,16,192]{3,2,1,0:T(8,128)(2,1)S(1)}, bf16[8,2,16,192]{3,2,1,0:T(8,128)(2,1)S(1)}, u32[]{:S(2)}, u32[]{:S(2)}) %collective-permute-start.2) | collective-permute-done | bytes 98336 | tf_op jit(solution)/shard_map/while/body/eval_jaxpr/ppermute | solution.py:48
  91.6 1.9 %collective-permute-start = (bf16[10,1,16,192]{3,2,1,0:T(8,128)(2,1)S(1)}, bf16[10,1,16,192]{3,2,1,0:T(8,128)(2,1)S(1)}, u32[]{:S(2)}, u32[]{:S(2)}) collective-permute-start(bf16[10,1,16,192]{3,2,1,0:T(8,128)(2,1)S(1)} %get-tuple-element.315), channel_id=1, source_target_pairs={{1,0},{2,1},{3,2},{4,3},{5,4},{6,5},{7,6},{9,8},{10,9},{11,10},{12... | collective-permute-start | bytes 184328 | tf_op jit(solution)/shard_map/while/body/eval_jaxpr/ppermute | solution.py:40
  93.6 2.4 %collective-permute-start.1 = (bf16[10,1,16,192]{3,2,1,0:T(8,128)(2,1)S(1)}, bf16[10,1,16,192]{3,2,1,0:T(8,128)(2,1)S(1)}, u32[]{:S(2)}, u32[]{:S(2)}) collective-permute-start(bf16[10,1,16,192]{3,2,1,0:T(8,128)(2,1)S(1)} %get-tuple-element.316), channel_id=1, source_target_pairs={{0,1},{1,2},{2,3},{3,4},{4,5},{5,6},{6,7},{8,9},{9,10},{10,11},{11... | collective-permute-start | bytes 184328 | tf_op jit(solution)/shard_map/while/body/eval_jaxpr/ppermute | solution.py:37
  96.0 3.3 %collective-permute-done.1 = bf16[10,1,16,192]{3,2,1,0:T(8,128)(2,1)S(1)} collective-permute-done((bf16[10,1,16,192]{3,2,1,0:T(8,128)(2,1)S(1)}, bf16[10,1,16,192]{3,2,1,0:T(8,128)(2,1)S(1)}, u32[]{:S(2)}, u32[]{:S(2)}) %collective-permute-start.1) | collective-permute-done | bytes 61472 | tf_op jit(solution)/shard_map/while/body/eval_jaxpr/ppermute | solution.py:37
  99.4 4.4 %collective-permute-start.2 = (bf16[8,2,16,192]{3,2,1,0:T(8,128)(2,1)S(1)}, bf16[8,2,16,192]{3,2,1,0:T(8,128)(2,1)S(1)}, u32[]{:S(2)}, u32[]{:S(2)}) collective-permute-start(bf16[8,2,16,192]{3,2,1,0:T(8,128)(2,1)S(1)} %get-tuple-element.363), channel_id=1, source_target_pairs={{0,8},{8,16},{16,24},{1,9},{9,17},{17,25},{2,10},{10,18},{18,26},{... | collective-permute-start | bytes 294920 | tf_op jit(solution)/shard_map/while/body/eval_jaxpr/ppermute | solution.py:48
  105.4 1.8 %collective-permute-done.2 = bf16[8,2,16,192]{3,2,1,0:T(8,128)(2,1)S(1)} collective-permute-done((bf16[8,2,16,192]{3,2,1,0:T(8,128)(2,1)S(1)}, bf16[8,2,16,192]{3,2,1,0:T(8,128)(2,1)S(1)}, u32[]{:S(2)}, u32[]{:S(2)}) %collective-permute-start.2) | collective-permute-done | bytes 98336 | tf_op jit(solution)/shard_map/while/body/eval_jaxpr/ppermute | solution.py:48
  111.0 1.9 %collective-permute-start = (bf16[10,1,16,192]{3,2,1,0:T(8,128)(2,1)S(1)}, bf16[10,1,16,192]{3,2,1,0:T(8,128)(2,1)S(1)}, u32[]{:S(2)}, u32[]{:S(2)}) collective-permute-start(bf16[10,1,16,192]{3,2,1,0:T(8,128)(2,1)S(1)} %get-tuple-element.315), channel_id=1, source_target_pairs={{1,0},{2,1},{3,2},{4,3},{5,4},{6,5},{7,6},{9,8},{10,9},{11,10},{12... | collective-permute-start | bytes 184328 | tf_op jit(solution)/shard_map/while/body/eval_jaxpr/ppermute | solution.py:40
  113.0 2.4 %collective-permute-start.1 = (bf16[10,1,16,192]{3,2,1,0:T(8,128)(2,1)S(1)}, bf16[10,1,16,192]{3,2,1,0:T(8,128)(2,1)S(1)}, u32[]{:S(2)}, u32[]{:S(2)}) collective-permute-start(bf16[10,1,16,192]{3,2,1,0:T(8,128)(2,1)S(1)} %get-tuple-element.316), channel_id=1, source_target_pairs={{0,1},{1,2},{2,3},{3,4},{4,5},{5,6},{6,7},{8,9},{9,10},{10,11},{11... | collective-permute-start | bytes 184328 | tf_op jit(solution)/shard_map/while/body/eval_jaxpr/ppermute | solution.py:37
  115.4 3.3 %collective-permute-done.1 = bf16[10,1,16,192]{3,2,1,0:T(8,128)(2,1)S(1)} collective-permute-done((bf16[10,1,16,192]{3,2,1,0:T(8,128)(2,1)S(1)}, bf16[10,1,16,192]{3,2,1,0:T(8,128)(2,1)S(1)}, u32[]{:S(2)}, u32[]{:S(2)}) %collective-permute-start.1) | collective-permute-done | bytes 61472 | tf_op jit(solution)/shard_map/while/body/eval_jaxpr/ppermute | solution.py:37
  118.8 12.7 %collective-permute-start.2 = (bf16[8,2,16,192]{3,2,1,0:T(8,128)(2,1)S(1)}, bf16[8,2,16,192]{3,2,1,0:T(8,128)(2,1)S(1)}, u32[]{:S(2)}, u32[]{:S(2)}) collective-permute-start(bf16[8,2,16,192]{3,2,1,0:T(8,128)(2,1)S(1)} %get-tuple-element.363), channel_id=1, source_target_pairs={{0,8},{8,16},{16,24},{1,9},{9,17},{17,25},{2,10},{10,18},{18,26},{... | collective-permute-start | bytes 294920 | tf_op jit(solution)/shard_map/while/body/eval_jaxpr/ppermute | solution.py:48
  133.1 1.8 %collective-permute-done.2 = bf16[8,2,16,192]{3,2,1,0:T(8,128)(2,1)S(1)} collective-permute-done((bf16[8,2,16,192]{3,2,1,0:T(8,128)(2,1)S(1)}, bf16[8,2,16,192]{3,2,1,0:T(8,128)(2,1)S(1)}, u32[]{:S(2)}, u32[]{:S(2)}) %collective-permute-start.2) | collective-permute-done | bytes 98336 | tf_op jit(solution)/shard_map/while/body/eval_jaxpr/ppermute | solution.py:48
  135.9 14.7 %collective-permute-start.5 = (bf16[1,1,4,2,16,192]{5,4,3,2,1,0:T(8,128)(2,1)S(1)}, bf16[1,1,4,2,16,192]{5,4,3,2,1,0:T(8,128)(2,1)S(1)}, u32[]{:S(2)}, u32[]{:S(2)}) collective-permute-start(bf16[1,1,4,2,16,192]{5,4,3,2,1,0:T(8,128)(2,1)S(1)} %get-tuple-element.230), channel_id=1, source_target_pairs={{0,24},{8,16},{16,8},{24,0},{1,25},{9,17},{17,9},{25,1},{2,26},{10... | collective-permute-start | bytes 147464 | tf_op jit(solution)/shard_map/ppermute | solution.py:27
  151.2 1.9 %collective-permute-done.5 = bf16[1,1,4,2,16,192]{5,4,3,2,1,0:T(8,128)(2,1)S(1)} collective-permute-done((bf16[1,1,4,2,16,192]{5,4,3,2,1,0:T(8,128)(2,1)S(1)}, bf16[1,1,4,2,16,192]{5,4,3,2,1,0:T(8,128)(2,1)S(1)}, u32[]{:S(2)}, u32[]{:S(2)}) %collective-permute-start.5) | collective-permute-done | bytes 49184 | tf_op jit(solution)/shard_map/ppermute | solution.py:27
  153.1 2.7 %collective-permute-done.4 = bf16[1,1,4,2,16,192]{5,4,3,2,1,0:T(8,128)(2,1)S(1)} collective-permute-done((bf16[1,1,4,2,16,192]{5,4,3,2,1,0:T(8,128)(2,1)S(1)}, bf16[1,1,4,2,16,192]{5,4,3,2,1,0:T(8,128)(2,1)S(1)}, u32[]{:S(2)}, u32[]{:S(2)}) %collective-permute-start.4) | collective-permute-done | bytes 49184 | tf_op jit(solution)/shard_map/ppermute | solution.py:27
  (84 shorter events, 43.8 us)
Async XLA Ops:
  4.6 4.4 %collective-permute-start = (bf16[10,1,16,192]{3,2,1,0:T(8,128)(2,1)S(1)}, bf16[10,1,16,192]{3,2,1,0:T(8,128)(2,1)S(1)}, u32[]{:S(2)}, u32[]{:S(2)}) collective-permute-start(bf16[10,1,16,192]{3,2,1,0:T(8,128)(2,1)S(1)} %get-tuple-element.315), channel_id=1, source_target_pairs={{1,0},{2,1},{3,2},{4,3},{5,4},{6,5},{7,6},{9,8},{10,9},{11,10},{12... | collective-permute-start | bytes 184328 | tf_op jit(solution)/shard_map/while/body/eval_jaxpr/ppermute | solution.py:40
  6.5 5.8 %collective-permute-start.1 = (bf16[10,1,16,192]{3,2,1,0:T(8,128)(2,1)S(1)}, bf16[10,1,16,192]{3,2,1,0:T(8,128)(2,1)S(1)}, u32[]{:S(2)}, u32[]{:S(2)}) collective-permute-start(bf16[10,1,16,192]{3,2,1,0:T(8,128)(2,1)S(1)} %get-tuple-element.316), channel_id=1, source_target_pairs={{0,1},{1,2},{2,3},{3,4},{4,5},{5,6},{6,7},{8,9},{9,10},{10,11},{11... | collective-permute-start | bytes 184328 | tf_op jit(solution)/shard_map/while/body/eval_jaxpr/ppermute | solution.py:37
  20.7 2.4 %copy-start = (f32[1,192]{1,0:T(1,128)S(1)}, f32[1,192]{1,0:T(1,128)}, u32[]{:S(2)}) copy-start(f32[1,192]{1,0:T(1,128)} %get-tuple-element.113) | copy-start | bytes 2308 | tf_op jit(solution)/shard_map/while/body/eval_jaxpr/cond
  23.2 4.6 %collective-permute-start.2 = (bf16[8,2,16,192]{3,2,1,0:T(8,128)(2,1)S(1)}, bf16[8,2,16,192]{3,2,1,0:T(8,128)(2,1)S(1)}, u32[]{:S(2)}, u32[]{:S(2)}) collective-permute-start(bf16[8,2,16,192]{3,2,1,0:T(8,128)(2,1)S(1)} %get-tuple-element.363), channel_id=1, source_target_pairs={{0,8},{8,16},{16,24},{1,9},{9,17},{17,25},{2,10},{10,18},{18,26},{... | collective-permute-start | bytes 294920 | tf_op jit(solution)/shard_map/while/body/eval_jaxpr/ppermute | solution.py:48
  31.6 4.4 %collective-permute-start = (bf16[10,1,16,192]{3,2,1,0:T(8,128)(2,1)S(1)}, bf16[10,1,16,192]{3,2,1,0:T(8,128)(2,1)S(1)}, u32[]{:S(2)}, u32[]{:S(2)}) collective-permute-start(bf16[10,1,16,192]{3,2,1,0:T(8,128)(2,1)S(1)} %get-tuple-element.315), channel_id=1, source_target_pairs={{1,0},{2,1},{3,2},{4,3},{5,4},{6,5},{7,6},{9,8},{10,9},{11,10},{12... | collective-permute-start | bytes 184328 | tf_op jit(solution)/shard_map/while/body/eval_jaxpr/ppermute | solution.py:40
  33.5 5.8 %collective-permute-start.1 = (bf16[10,1,16,192]{3,2,1,0:T(8,128)(2,1)S(1)}, bf16[10,1,16,192]{3,2,1,0:T(8,128)(2,1)S(1)}, u32[]{:S(2)}, u32[]{:S(2)}) collective-permute-start(bf16[10,1,16,192]{3,2,1,0:T(8,128)(2,1)S(1)} %get-tuple-element.316), channel_id=1, source_target_pairs={{0,1},{1,2},{2,3},{3,4},{4,5},{5,6},{6,7},{8,9},{9,10},{10,11},{11... | collective-permute-start | bytes 184328 | tf_op jit(solution)/shard_map/while/body/eval_jaxpr/ppermute | solution.py:37
  47.7 2.4 %copy-start = (f32[1,192]{1,0:T(1,128)S(1)}, f32[1,192]{1,0:T(1,128)}, u32[]{:S(2)}) copy-start(f32[1,192]{1,0:T(1,128)} %get-tuple-element.113) | copy-start | bytes 2308 | tf_op jit(solution)/shard_map/while/body/eval_jaxpr/cond
  50.1 7.5 %collective-permute-start.2 = (bf16[8,2,16,192]{3,2,1,0:T(8,128)(2,1)S(1)}, bf16[8,2,16,192]{3,2,1,0:T(8,128)(2,1)S(1)}, u32[]{:S(2)}, u32[]{:S(2)}) collective-permute-start(bf16[8,2,16,192]{3,2,1,0:T(8,128)(2,1)S(1)} %get-tuple-element.363), channel_id=1, source_target_pairs={{0,8},{8,16},{16,24},{1,9},{9,17},{17,25},{2,10},{10,18},{18,26},{... | collective-permute-start | bytes 294920 | tf_op jit(solution)/shard_map/while/body/eval_jaxpr/ppermute | solution.py:48
  61.5 4.4 %collective-permute-start = (bf16[10,1,16,192]{3,2,1,0:T(8,128)(2,1)S(1)}, bf16[10,1,16,192]{3,2,1,0:T(8,128)(2,1)S(1)}, u32[]{:S(2)}, u32[]{:S(2)}) collective-permute-start(bf16[10,1,16,192]{3,2,1,0:T(8,128)(2,1)S(1)} %get-tuple-element.315), channel_id=1, source_target_pairs={{1,0},{2,1},{3,2},{4,3},{5,4},{6,5},{7,6},{9,8},{10,9},{11,10},{12... | collective-permute-start | bytes 184328 | tf_op jit(solution)/shard_map/while/body/eval_jaxpr/ppermute | solution.py:40
  63.4 5.8 %collective-permute-start.1 = (bf16[10,1,16,192]{3,2,1,0:T(8,128)(2,1)S(1)}, bf16[10,1,16,192]{3,2,1,0:T(8,128)(2,1)S(1)}, u32[]{:S(2)}, u32[]{:S(2)}) collective-permute-start(bf16[10,1,16,192]{3,2,1,0:T(8,128)(2,1)S(1)} %get-tuple-element.316), channel_id=1, source_target_pairs={{0,1},{1,2},{2,3},{3,4},{4,5},{5,6},{6,7},{8,9},{9,10},{10,11},{11... | collective-permute-start | bytes 184328 | tf_op jit(solution)/shard_map/while/body/eval_jaxpr/ppermute | solution.py:37
  69.2 18.5 %collective-permute-start.2 = (bf16[8,2,16,192]{3,2,1,0:T(8,128)(2,1)S(1)}, bf16[8,2,16,192]{3,2,1,0:T(8,128)(2,1)S(1)}, u32[]{:S(2)}, u32[]{:S(2)}) collective-permute-start(bf16[8,2,16,192]{3,2,1,0:T(8,128)(2,1)S(1)} %get-tuple-element.363), channel_id=1, source_target_pairs={{0,8},{8,16},{16,24},{1,9},{9,17},{17,25},{2,10},{10,18},{18,26},{... | collective-permute-start | bytes 294920 | tf_op jit(solution)/shard_map/while/body/eval_jaxpr/ppermute | solution.py:48
  91.6 4.4 %collective-permute-start = (bf16[10,1,16,192]{3,2,1,0:T(8,128)(2,1)S(1)}, bf16[10,1,16,192]{3,2,1,0:T(8,128)(2,1)S(1)}, u32[]{:S(2)}, u32[]{:S(2)}) collective-permute-start(bf16[10,1,16,192]{3,2,1,0:T(8,128)(2,1)S(1)} %get-tuple-element.315), channel_id=1, source_target_pairs={{1,0},{2,1},{3,2},{4,3},{5,4},{6,5},{7,6},{9,8},{10,9},{11,10},{12... | collective-permute-start | bytes 184328 | tf_op jit(solution)/shard_map/while/body/eval_jaxpr/ppermute | solution.py:40
  93.6 5.8 %collective-permute-start.1 = (bf16[10,1,16,192]{3,2,1,0:T(8,128)(2,1)S(1)}, bf16[10,1,16,192]{3,2,1,0:T(8,128)(2,1)S(1)}, u32[]{:S(2)}, u32[]{:S(2)}) collective-permute-start(bf16[10,1,16,192]{3,2,1,0:T(8,128)(2,1)S(1)} %get-tuple-element.316), channel_id=1, source_target_pairs={{0,1},{1,2},{2,3},{3,4},{4,5},{5,6},{6,7},{8,9},{9,10},{10,11},{11... | collective-permute-start | bytes 184328 | tf_op jit(solution)/shard_map/while/body/eval_jaxpr/ppermute | solution.py:37
  99.4 7.8 %collective-permute-start.2 = (bf16[8,2,16,192]{3,2,1,0:T(8,128)(2,1)S(1)}, bf16[8,2,16,192]{3,2,1,0:T(8,128)(2,1)S(1)}, u32[]{:S(2)}, u32[]{:S(2)}) collective-permute-start(bf16[8,2,16,192]{3,2,1,0:T(8,128)(2,1)S(1)} %get-tuple-element.363), channel_id=1, source_target_pairs={{0,8},{8,16},{16,24},{1,9},{9,17},{17,25},{2,10},{10,18},{18,26},{... | collective-permute-start | bytes 294920 | tf_op jit(solution)/shard_map/while/body/eval_jaxpr/ppermute | solution.py:48
  111.0 4.4 %collective-permute-start = (bf16[10,1,16,192]{3,2,1,0:T(8,128)(2,1)S(1)}, bf16[10,1,16,192]{3,2,1,0:T(8,128)(2,1)S(1)}, u32[]{:S(2)}, u32[]{:S(2)}) collective-permute-start(bf16[10,1,16,192]{3,2,1,0:T(8,128)(2,1)S(1)} %get-tuple-element.315), channel_id=1, source_target_pairs={{1,0},{2,1},{3,2},{4,3},{5,4},{6,5},{7,6},{9,8},{10,9},{11,10},{12... | collective-permute-start | bytes 184328 | tf_op jit(solution)/shard_map/while/body/eval_jaxpr/ppermute | solution.py:40
  113.0 5.8 %collective-permute-start.1 = (bf16[10,1,16,192]{3,2,1,0:T(8,128)(2,1)S(1)}, bf16[10,1,16,192]{3,2,1,0:T(8,128)(2,1)S(1)}, u32[]{:S(2)}, u32[]{:S(2)}) collective-permute-start(bf16[10,1,16,192]{3,2,1,0:T(8,128)(2,1)S(1)} %get-tuple-element.316), channel_id=1, source_target_pairs={{0,1},{1,2},{2,3},{3,4},{4,5},{5,6},{6,7},{8,9},{9,10},{10,11},{11... | collective-permute-start | bytes 184328 | tf_op jit(solution)/shard_map/while/body/eval_jaxpr/ppermute | solution.py:37
  118.8 16.1 %collective-permute-start.2 = (bf16[8,2,16,192]{3,2,1,0:T(8,128)(2,1)S(1)}, bf16[8,2,16,192]{3,2,1,0:T(8,128)(2,1)S(1)}, u32[]{:S(2)}, u32[]{:S(2)}) collective-permute-start(bf16[8,2,16,192]{3,2,1,0:T(8,128)(2,1)S(1)} %get-tuple-element.363), channel_id=1, source_target_pairs={{0,8},{8,16},{16,24},{1,9},{9,17},{17,25},{2,10},{10,18},{18,26},{... | collective-permute-start | bytes 294920 | tf_op jit(solution)/shard_map/while/body/eval_jaxpr/ppermute | solution.py:48
  135.9 17.2 %collective-permute-start.5 = (bf16[1,1,4,2,16,192]{5,4,3,2,1,0:T(8,128)(2,1)S(1)}, bf16[1,1,4,2,16,192]{5,4,3,2,1,0:T(8,128)(2,1)S(1)}, u32[]{:S(2)}, u32[]{:S(2)}) collective-permute-start(bf16[1,1,4,2,16,192]{5,4,3,2,1,0:T(8,128)(2,1)S(1)} %get-tuple-element.230), channel_id=1, source_target_pairs={{0,24},{8,16},{16,8},{24,0},{1,25},{9,17},{17,9},{25,1},{2,26},{10... | collective-permute-start | bytes 147464 | tf_op jit(solution)/shard_map/ppermute | solution.py:27
  150.5 5.3 %collective-permute-start.4 = (bf16[1,1,4,2,16,192]{5,4,3,2,1,0:T(8,128)(2,1)S(1)}, bf16[1,1,4,2,16,192]{5,4,3,2,1,0:T(8,128)(2,1)S(1)}, u32[]{:S(2)}, u32[]{:S(2)}) collective-permute-start(bf16[1,1,4,2,16,192]{5,4,3,2,1,0:T(8,128)(2,1)S(1)} %get-tuple-element.231), channel_id=1, source_target_pairs={{0,16},{8,24},{16,0},{24,8},{1,17},{9,25},{17,1},{25,9},{2,18},{10... | collective-permute-start | bytes 147464 | tf_op jit(solution)/shard_map/ppermute | solution.py:27
  150.5 5.3 %collective-permute-start.3 = (bf16[1,1,4,2,16,192]{5,4,3,2,1,0:T(8,128)(2,1)S(1)}, bf16[1,1,4,2,16,192]{5,4,3,2,1,0:T(8,128)(2,1)S(1)}, u32[]{:S(2)}, u32[]{:S(2)}) collective-permute-start(bf16[1,1,4,2,16,192]{5,4,3,2,1,0:T(8,128)(2,1)S(1)} %get-tuple-element.232), channel_id=1, source_target_pairs={{0,8},{8,0},{16,24},{24,16},{1,9},{9,1},{17,25},{25,17},{2,10},{10... | collective-permute-start | bytes 147464 | tf_op jit(solution)/shard_map/ppermute | solution.py:27
